TPU v7x, 512 devices: a whole 4x4x16 slice. The times are simulated.
512 devices in a mesh: pack: 16 (over y, x), seq: 32 (over z, core).
Axes of the slice: x: 4, y: 4, z: 16, core: 2. Of those that a mesh axis runs over, the one named last changes fastest.
Arguments:
- queries: bfloat16 [65536, 2048], P(('pack', 'seq')), parts along dimension 0, may hold values from -48 to 48
- token_key_heads: bfloat16 [65536, 256], P(('pack', 'seq')), parts along dimension 0, may hold values from -6 to 6
- token_value_heads: bfloat16 [65536, 256], P(('pack', 'seq')), parts along dimension 0, may hold values from -6 to 6
- residual: bfloat16 [65536, 1024], P(('pack', 'seq')), parts along dimension 0, may hold values from -40 to 40
- out_weight: bfloat16 [2048, 1024], P('seq'), may hold values from -0.125 to 0.125
- norm_gain: bfloat16 [1024], replicated, may hold values from 0.5 to 1.5
- w_gate: bfloat16 [32, 1024, 384], P('seq'), may hold values from -0.1875 to 0.1875
- w_up: bfloat16 [32, 1024, 384], P('seq'), may hold values from -0.1875 to 0.1875
- w_down: bfloat16 [32, 384, 1024], P('seq'), may hold values from -0.3125 to 0.3125
- expert_ids: int32 [65536, 8], P(('pack', 'seq')), parts along dimension 0, may hold values from 0 to 31, all different within a row; in each aligned block of 128 rows (0 to 127, 128 to 255, ...) at most 48 rows name the same one
- gate_weights: float32 [65536, 8], P(('pack', 'seq')), parts along dimension 0, may hold values from 0.05 to 0.3
- doc_of_block: int32 [512], P('pack'), parts along dimension 0, may hold values from 0 to 7, never falling along the last dimension, each value on 1 to 8 neighbouring positions
Outputs:
- attention: bfloat16 [65536, 2048], P(('pack', 'seq')), parts along dimension 0
- hidden_out: bfloat16 [65536, 1024], P(('pack', 'seq')), parts along dimension 0
- expert_mix: bfloat16 [65536, 1024], P(('pack', 'seq')), parts along dimension 0
There are 16 independent parts, one for each index of `pack`. A program takes and returns all parts, laid end to end along the dimension named above; an argument that names none is the same for every part. Nothing has to cross between parts.
Inputs may be any that keep to these rules, and one draw needn't show every extreme that they name: `expert_ids`: each row names 8 different experts; within the rows of one block no expert is named more than 48 times, and in every draw some expert is named exactly 48 times by the rows of some block. `doc_of_block`: never falls from block to block; each document covers 1 to 8 blocks, one exactly 8.
All inputs are finite; a program needn't handle non-finite values.
Results may differ from a plain program's by a relative error of at most 0.015.
Values may be sent and summed in bfloat16 or wider, within the bound.
A program may use at most 64 MiB of HBM per device.

v0:
```python
import math
import jax
import jax.numpy as jnp
from jax import lax
from jax.sharding import PartitionSpec as P

QUERY_HEADS = 16
KEY_VALUE_HEADS = 2
HEAD_SIZE = 128
TOP = 8


def attend(queries, key_token_rows, value_token_rows, query_pos, key_pos, allowed):
    token_rows = queries.shape[0]
    heads_per_group = QUERY_HEADS // KEY_VALUE_HEADS
    token_query_heads = queries.reshape(token_rows, KEY_VALUE_HEADS, heads_per_group, HEAD_SIZE)
    key_count = key_token_rows.shape[0]
    tile_length = math.gcd(key_count, 512)
    number_of_tiles = key_count // tile_length
    key_tile_list = key_token_rows.reshape(number_of_tiles, tile_length, KEY_VALUE_HEADS, HEAD_SIZE)
    value_tile_list = value_token_rows.reshape(
        number_of_tiles, tile_length, KEY_VALUE_HEADS, HEAD_SIZE
    )
    pos_tiles = key_pos.reshape(number_of_tiles, tile_length)
    allowed_tiles = allowed.reshape(number_of_tiles, tile_length)
    factor = 1.0 / HEAD_SIZE**0.5

    def tile_step(running, tile):
        key_tile, value_tile, pos_tile, allowed_tile = tile
        visible = allowed_tile[None, :] & (pos_tile[None, :] <= query_pos[:, None])

        def compute(current):
            run_max, run_sum, accum = current
            scores = (
                jnp.einsum(
                    "tkgd,skd->kgts",
                    token_query_heads,
                    key_tile,
                    preferred_element_type=jnp.float32,
                )
                * factor
            )
            scores = jnp.where(visible, scores, -1e30)
            new_max = jnp.maximum(run_max, jnp.max(scores, axis=-1))
            terms = jnp.where(visible, jnp.exp(scores - new_max[..., None]), 0.0)
            rescale = jnp.exp(run_max - new_max)
            new_sum = run_sum * rescale + jnp.sum(terms, axis=-1)
            product = jnp.einsum(
                "kgts,skd->kgtd",
                terms.astype(jnp.bfloat16),
                value_tile,
                preferred_element_type=jnp.float32,
            )
            return (new_max, new_sum, accum * rescale[..., None] + product)

        return (lax.cond(jnp.any(visible), compute, lambda current: current, running), None)

    start_state = (
        jnp.full((KEY_VALUE_HEADS, heads_per_group, token_rows), -1e30, jnp.float32),
        jnp.zeros((KEY_VALUE_HEADS, heads_per_group, token_rows), jnp.float32),
        jnp.zeros((KEY_VALUE_HEADS, heads_per_group, token_rows, HEAD_SIZE), jnp.float32),
    )
    final_state, _ = lax.scan(
        tile_step, start_state, (key_tile_list, value_tile_list, pos_tiles, allowed_tiles)
    )
    run_max, run_sum, accum = final_state
    result = accum / run_sum[..., None]
    return (
        jnp.transpose(result, (2, 0, 1, 3))
        .reshape(token_rows, QUERY_HEADS * HEAD_SIZE)
        .astype(jnp.bfloat16)
    )


def expert_rows(arrived, gate_proj, up_proj, down_proj):
    sources, slot_count, width = arrived.shape
    flat_rows = arrived.reshape(sources * slot_count, width)
    gate_part = jnp.dot(flat_rows, gate_proj, preferred_element_type=jnp.float32)
    up_part = jnp.dot(flat_rows, up_proj, preferred_element_type=jnp.float32)
    activated = (jax.nn.silu(gate_part) * up_part).astype(jnp.bfloat16)
    produced = jnp.dot(activated, down_proj, preferred_element_type=jnp.float32).astype(
        jnp.bfloat16
    )
    return produced.reshape(sources, slot_count, width)


def shards(
    queries,
    token_key_heads,
    token_value_heads,
    residual,
    out_weight,
    norm_gain,
    w_gate,
    w_up,
    w_down,
    expert_ids,
    gate_weights,
    doc_of_block,
):
    token_rows = queries.shape[0]
    blocks = lax.axis_size("seq")
    own_index = lax.axis_index("seq")
    local_pos = jnp.arange(token_rows, dtype=jnp.int32)
    query_pos = own_index * token_rows + local_pos
    own_doc = doc_of_block[own_index]
    key_head_width = token_key_heads.shape[1]
    key_token_rows, value_token_rows = (
        lax.all_gather(token_key_heads, "seq", axis=0, tiled=True),
        lax.all_gather(token_value_heads, "seq", axis=0, tiled=True),
    )
    key_pos = jnp.arange(blocks * token_rows, dtype=jnp.int32)
    key_block = key_pos // token_rows
    allowed = (key_block <= own_index) & ((doc_of_block[key_block] == own_doc) | (key_block == 0))
    key_token_rows = key_token_rows.reshape(
        key_token_rows.shape[0], KEY_VALUE_HEADS, key_head_width // KEY_VALUE_HEADS
    )
    value_token_rows = value_token_rows.reshape(
        value_token_rows.shape[0], KEY_VALUE_HEADS, key_head_width // KEY_VALUE_HEADS
    )
    attention = attend(queries, key_token_rows, value_token_rows, query_pos, key_pos, allowed)
    width = residual.shape[1]
    projected = jnp.dot(
        attention,
        lax.all_gather(out_weight, "seq", axis=0, tiled=True),
        preferred_element_type=jnp.float32,
    )
    hidden_state = residual.astype(jnp.float32) + projected
    mean_square = jnp.mean(hidden_state * hidden_state, axis=-1, keepdims=True)
    normed = (hidden_state * lax.rsqrt(mean_square + 1e-06) * norm_gain.astype(jnp.float32)).astype(
        jnp.bfloat16
    )
    slot_cap = min(token_rows, 3 * token_rows * TOP // (2 * blocks))
    routed_ids = expert_ids.reshape(-1)
    one_hot = (routed_ids[:, None] == jnp.arange(blocks, dtype=jnp.int32)[None, :]).astype(
        jnp.int32
    )
    earlier = jnp.cumsum(one_hot, axis=0) - one_hot
    slot_pos = jnp.sum(earlier * one_hot, axis=1)
    slot_index = routed_ids * slot_cap + slot_pos
    token_of = jnp.arange(token_rows * TOP, dtype=jnp.int32) // TOP
    outgoing = (
        jnp.zeros((blocks * slot_cap, width), jnp.bfloat16).at[slot_index].set(normed[token_of])
    )
    outgoing = outgoing.reshape(blocks, slot_cap, width)
    arrived = lax.all_to_all(outgoing, "seq", split_axis=0, concat_axis=0, tiled=True)
    served = expert_rows(arrived, w_gate[0], w_up[0], w_down[0])
    returned_rows = lax.all_to_all(served, "seq", split_axis=0, concat_axis=0, tiled=True)
    picked = returned_rows.reshape(blocks * slot_cap, width)[slot_index].astype(jnp.float32)
    weighted = picked * gate_weights.reshape(-1)[:, None]
    expert_mix = jnp.sum(weighted.reshape(token_rows, TOP, width), axis=1).astype(jnp.bfloat16)
    return (attention, hidden_state.astype(jnp.bfloat16), expert_mix)


def solution(mesh):
    in_specs = (
        P(("pack", "seq"), None),
        P(("pack", "seq"), None),
        P(("pack", "seq"), None),
        P(("pack", "seq"), None),
        P("seq", None),
        P(),
        P("seq", None, None),
        P("seq", None, None),
        P("seq", None, None),
        P(("pack", "seq"), None),
        P(("pack", "seq"), None),
        P("pack"),
    )
    out_specs = (P(("pack", "seq"), None), P(("pack", "seq"), None), P(("pack", "seq"), None))
    return jax.shard_map(shards, mesh=mesh, in_specs=in_specs, out_specs=out_specs, check_vma=False)
```

profile of v0, /device:TPU:4, one launch (start us, length us, event | category | flops | bytes accessed | tf_op | source)
XLA Modules:
  0.0 583.3 jit_solution(16247242193508925619)
XLA Ops:
  11.9 1.9 fusion.43
  13.8 2.1 fusion.42
  15.8 4.5 compare_select_fusion.1
  20.3 16.1 %select_compare_fusion = pred[4096]{0:T(1024)(128)(4,1)S(1)} fusion(pred[4096]{0:T(1024)(128)(4,1)S(1)} %compare_reduce_fusion, pred[4096]{0:T(1024)(128)(4,1)S(1)} %compare_reduce_fusion.1, pred[4096]{0:T(1024)(128)(4,1)S(1)} %compare_reduce_fusion.2, pred[4096]{0:T(1024)(128)(4,1)S(1)} %compare_reduce_fusion.3, ...), kind=kLoop, calls=%fused_computation.99 | loop fusion | flops 106496 | bytes 122984 | tf_op jit(solution)/shard_map/eq | solution.py:114
  38.8 9.0 %reduce-window.6 = s32[32,8,128]{2,1,0:T(8,128)S(1)} reduce-window(s32[32,8,128]{2,1,0:T(8,128)S(1)} %fusion.37, s32[]{:T(128)} %copy.62), window={size=1x1x128 pad=0_0x0_0x127_0}, to_apply=%region_7.8 | reduce-window | flops 4161536 | bytes 262148 | tf_op jit(solution)/shard_map/reduce-window
  48.6 37.9 %all-gather.4.cloned.1.call-done = bf16[4096,256]{1,0:T(8,128)(2,1)} async-done(((bf16[128,256]{1,0:T(8,128)(2,1)}), bf16[4096,256]{1,0:T(8,128)(2,1)}) %all-gather.4.cloned.1.call-update) | async-done | bytes 2097168 | tf_op jit(solution)/shard_map/all_gather | solution.py:109
  86.5 2.5 reshape.356
  89.0 1.8 copy.22
  90.8 66.5 %all-gather.6.cloned.1.call-done = bf16[4096,256]{1,0:T(8,128)(2,1)} async-done(((bf16[128,256]{1,0:T(8,128)(2,1)}), bf16[4096,256]{1,0:T(8,128)(2,1)}) %all-gather.6.cloned.1.call-update) | async-done | bytes 2097168 | tf_op jit(solution)/shard_map/all_gather | solution.py:110
  157.3 2.5 reshape.357
  159.9 1.8 copy.24
  161.7 18.0 %while.15 = (s32[]{:T(128)}, f32[2,8,128]{2,1,0:T(8,128)S(1)}, f32[2,8,128]{2,1,0:T(8,128)S(1)}, f32[2,8,128,128]{3,2,1,0:T(8,128)S(1)}, pred[8,512]{1,0:T(8,128...) while((s32[]{:T(128)}, f32[2,8,128]{2,1,0:T(8,128)S(1)}, ...), condition=%wide.region_6.7_spmd.clone, body=%wide.region_0.6_spmd.clone.sunk | while | flops 551227520 | bytes 16131831 | solution.py:63
  163.3 5.4 conditional.3
  166.0 2.6 fusion.8
  180.7 49.5 %all-gather.8.cloned.1.call-done = bf16[2048,1024]{1,0:T(8,128)(2,1)} async-done(((bf16[64,1024]{1,0:T(8,128)(2,1)}), bf16[2048,1024]{1,0:T(8,128)(2,1)}) %all-gather.8.cloned.1.call-update) | async-done | bytes 4194320 | tf_op jit(solution)/shard_map/all_gather | solution.py:125
  230.1 3.0 multiply_reduce_fusion
  233.9 14.9 %scatter_custom_fusion = bf16[1536,1024]{1,0:T(8,128)(2,1)} fusion(s32[1024]{0:T(1024)S(1)} %bitcast.128, bf16[128,1024]{1,0:T(8,128)(2,1)S(1)} %get-tuple-element.196, s32[1024]{0:T(1024)S(1)} %broadcast_clamp_fusion.1, bf16[]{:T(256)} %constant.107.clone.1), kind=kCustom, calls=%fused_computation.34 | custom fusion | bytes 3145730 | tf_op jit(solution)/shard_map/scatter | solution.py:143
  248.9 154.5 %all_to_all.10 = bf16[32,48,1024]{2,1,0:T(8,128)(2,1)S(1)} all-to-all(bf16[32,48,1024]{2,1,0:T(8,128)(2,1)} %bitcast.115), channel_id=1, replica_groups=mesh['pack'=16,'seq'=32] {'seq'}, dimensions={0} | all-to-all | bytes 6291456 | tf_op jit(solution)/shard_map/all_to_all | solution.py:146
  405.1 3.2 fusion.31
  408.3 7.8 %convolution_convert_fusion = bf16[1536,1024]{1,0:T(8,128)(2,1)} fusion(bf16[1536,1024]{1,0:T(8,128)(2,1)} %bitcast.118, f32[1536,384]{1,0:T(8,128)} %fusion.31, bf16[1,384,1024]{2,1,0:T(8,128)(2,1)S(1)} %copy-done, bf16[1,1024,384]{2,1,0:T(8,128)(2,1)S(1)} %copy-done.7), kind=kOutput, calls=%fused_computation.31 | convolution fusion | flops 2421030912 | bytes 10223616 | tf_op jit(solution)/shard_map/dot_general | solution.py:81
  416.1 4.9 all-to-all-start.1
  421.2 146.3 %all-to-all-done.1 = bf16[32,48,1024]{2,1,0:T(8,128)(2,1)} async-done(((bf16[32,48,1024]{2,1,0:T(8,128)(2,1)}), bf16[32,48,1024]{2,1,0:T(8,128)(2,1)}, u32[]{:S(2)}, u32[]{:S(2)}) %all-to-all-start.1) | async-done | bytes 3145760 | tf_op jit(solution)/shard_map/all_to_all | solution.py:148
  567.5 7.3 %gather_fusion = bf16[1024,1024]{1,0:T(8,128)(2,1)S(1)} fusion(bf16[1536,1024]{1,0:T(8,128)(2,1)} %bitcast.54, s32[1024]{0:T(1024)S(1)} %broadcast_clamp_fusion), kind=kCustom, calls=%fused_computation.1 | custom fusion | bytes 4198400 | tf_op jit(solution)/shard_map/gather | solution.py:149
  574.8 2.0 fusion.22
  (124 shorter events, 21.0 us)
Async XLA Ops:
  7.2 401.2 %copy-start = (bf16[1,384,1024]{2,1,0:T(8,128)(2,1)S(1)}, bf16[1,384,1024]{2,1,0:T(8,128)(2,1)}, u32[]{:S(2)}) copy-start(bf16[1,384,1024]{2,1,0:T(8,128)(2,1)} %param.24) | copy-start | bytes 2359300
  7.2 40.9 %copy-start.4 = (s32[128,8]{0,1:T(8,128)S(1)}, s32[128,8]{0,1:T(8,128)}, u32[]{:S(2)}) copy-start(s32[128,8]{0,1:T(8,128)} %param.25) | copy-start | bytes 12292
  7.2 79.3 %all-gather.4.cloned.1.call-start = ((), (), s32[]{:S(2)}) async-start(), calls=%async_computation.2 | async-start | bytes 2162688 | tf_op jit(solution)/shard_map/all_gather | solution.py:109
  7.9 149.4 %all-gather.6.cloned.1.call-start = ((), (), s32[]{:S(2)}) async-start(), calls=%async_computation.3 | async-start | bytes 2162688 | tf_op jit(solution)/shard_map/all_gather | solution.py:110
  8.7 221.5 %all-gather.8.cloned.1.call-start = ((), (), s32[]{:S(2)}) async-start(), calls=%async_computation.4 | async-start | bytes 4325376 | tf_op jit(solution)/shard_map/all_gather | solution.py:125
  179.8 50.4 %copy-start.3 = (bf16[128,1024]{1,0:T(8,128)(2,1)S(1)}, bf16[128,1024]{1,0:T(8,128)(2,1)}, u32[]{:S(2)}) copy-start(bf16[128,1024]{1,0:T(8,128)(2,1)} %param.19) | copy-start | bytes 786436
  180.6 53.3 %copy-start.2 = (bf16[16,8,16,128]{3,1,2,0:T(8,128)(2,1)}, bf16[16,8,16,128]{3,1,2,0:T(8,128)(2,1)S(1)}, u32[]{:S(2)}) copy-start(bf16[16,8,16,128]{3,1,2,0:T(8,128)(2,1)S(1)} %copy.43) | copy-start | bytes 1572868
  248.9 156.2 %copy-start.6 = (bf16[1,1024,384]{2,1,0:T(8,128)(2,1)S(1)}, bf16[1,1024,384]{2,1,0:T(8,128)(2,1)}, u32[]{:S(2)}) copy-start(bf16[1,1024,384]{2,1,0:T(8,128)(2,1)} %param.22) | copy-start | bytes 2359300
  403.4 1.7 copy-start.1
  405.1 3.3 copy-start.7
  416.1 5.0 copy-start.5
  416.1 151.3 %all-to-all-start.1 = ((bf16[32,48,1024]{2,1,0:T(8,128)(2,1)}), bf16[32,48,1024]{2,1,0:T(8,128)(2,1)}, u32[]{:S(2)}, u32[]{:S(2)}) async-start(bf16[32,48,1024]{2,1,0:T(8,128)(2,1)} %bitcast.116), calls=%async_computation.1 | async-start | bytes 6291456 | tf_op jit(solution)/shard_map/all_to_all | solution.py:148
Sparse Core Ops, SparseCore 0:
  10.1 76.2 all-gather.3
  88.6 68.6 all-gather.5
  159.4 70.6 all-gather.7
where the time goes:
time: 584 us; the launch traced here: 583 us
  waiting for transfers between devices  302 us (52%)
  blocking collectives  155 us (27%)
  other arithmetic  42.8 us (7%)
  local copies, waits for them, and re-layouts  40.6 us (7%)
  matrix products  18.4 us (3%)
  between operations  14 us (2%)
    all_to_all x1, blocking collectives, shards(): lax.all_to_all(outgoing, 'seq', split_axis=0, concat_axis=0, tiled=True)  155 us
    all_to_all x1, waiting for transfers between devices, shards(): lax.all_to_all(served, 'seq', split_axis=0, concat_axis=0, tiled=True)  146 us
    all_gather x1, waiting for transfers between devices, shards(): lax.all_gather(token_value_heads, 'seq', axis=0, tiled=True)  66.5 us
    all_gather x1, waiting for transfers between devices, shards(): lax.all_gather(out_weight, 'seq', axis=0, tiled=True)  49.5 us
    all_gather x1, waiting for transfers between devices, shards(): lax.all_gather(token_key_heads, 'seq', axis=0, tiled=True)  37.9 us
    eq x1, other arithmetic, shards(): doc_of_block[key_block] == own_doc  16.1 us
    scatter x1, local copies, waits for them, and re-layouts, shards(): jnp.zeros((blocks * slot_cap, width), jnp.bfloat16).at[slot_index]  14.9 us
  transfers between devices with their start and end apart: 4, of which 4 were waited for; matrix products, arithmetic and copies ran while one was open for 10% of the time, Pallas kernels for 0%

commit v1 on v0

--- a/solution.py
+++ b/solution.py
@@ -107,7 +107,10 @@
     key_head_width = token_key_heads.shape[1]
     key_token_rows, value_token_rows = (
         lax.all_gather(token_key_heads, "seq", axis=0, tiled=True),
-        lax.all_gather(token_value_heads, "seq", axis=0, tiled=True),
+        jnp.concatenate(
+            lax.all_to_all(jnp.stack([token_value_heads] * lax.axis_size("seq")), "seq", 0, 0),
+            axis=0,
+        ),
     )
     key_pos = jnp.arange(blocks * token_rows, dtype=jnp.int32)
     key_block = key_pos // token_rows

time: 584 us -> 561 us (0.961)
  waiting for transfers between devices: 302 us -> 230 us
  local copies, waits for them, and re-layouts: 40.6 us -> 60.9 us
  starting transfers between devices: 5.06 us -> 20.6 us
  other arithmetic: 42.8 us -> 54 us
    all_gather x1 -> x0, waiting for transfers between devices: 66.5 us -> none  [shards(): lax.all_gather(token_value_heads, 'seq', axis=0, tiled=True)]
    all_to_all x0 -> x1, starting transfers between devices: none -> 15.6 us  [shards(): lax.all_to_all(jnp.stack([token_value_heads] * lax.axis_size('seq')), 'se...]
    all_gather x1, waiting for transfers between devices: 49.5 us -> 35.4 us  [shards(): lax.all_gather(out_weight, 'seq', axis=0, tiled=True)]
    another operation x3, other arithmetic: 9.14 us -> 15.8 us
    all_to_all x0 -> x1, waiting for transfers between devices: none -> 6.13 us  [shards(): lax.all_to_all(jnp.stack([token_value_heads] * lax.axis_size('seq')), 'se...]
    unnamed x23 -> x32, local copies, waits for them, and re-layouts: 7.9 us -> 11.7 us
  transfers between devices with their start and end apart: 4 -> 4, of which waited for: 4 -> 4; matrix products, arithmetic and copies ran while one was open for 10% -> 17% of each run, Pallas kernels for 0% -> 0%
where the time goes in v1:
time: 561 us; the launch traced here: 558 us
  waiting for transfers between devices  230 us (41%)
  blocking collectives  154 us (27%)
  local copies, waits for them, and re-layouts  60.9 us (11%)
  other arithmetic  54 us (10%)
  starting transfers between devices  20.6 us (4%)
  matrix products  18.4 us (3%)
  between operations  14.3 us (3%)
    all_to_all x1, blocking collectives, shards(): lax.all_to_all(outgoing, 'seq', split_axis=0, concat_axis=0, tiled=True)  154 us
    all_to_all x1, waiting for transfers between devices, shards(): lax.all_to_all(served, 'seq', split_axis=0, concat_axis=0, tiled=True)  146 us
    all_gather x1, waiting for transfers between devices, shards(): lax.all_gather(token_key_heads, 'seq', axis=0, tiled=True)  41.2 us
    all_gather x1, waiting for transfers between devices, shards(): lax.all_gather(out_weight, 'seq', axis=0, tiled=True)  35.4 us
    eq x1, other arithmetic, shards(): doc_of_block[key_block] == own_doc  16.2 us
    another operation x3, other arithmetic  15.8 us
    all_to_all x1, starting transfers between devices, shards(): lax.all_to_all(jnp.stack([token_value_heads] * lax.axis_size('seq')), 'se...  15.6 us
    scatter x1, local copies, waits for them, and re-layouts, shards(): jnp.zeros((blocks * slot_cap, width), jnp.bfloat16).at[slot_index]  14.9 us
  transfers between devices with their start and end apart: 4, of which 4 were waited for; matrix products, arithmetic and copies ran while one was open for 17% of the time, Pallas kernels for 0%

profile of v1, /device:TPU:4, one launch (start us, length us, event | category | flops | bytes accessed | tf_op | source)
XLA Modules:
  0.0 558.2 jit_solution(9408962357878951327)
XLA Ops:
  10.7 15.6 %all-to-all-start = ((bf16[32,128,256]{1,2,0:T(8,128)(2,1)}), bf16[32,128,256]{1,2,0:T(8,128)(2,1)S(1)}, u32[]{:S(2)}, u32[]{:S(2)}) async-start(bf16[32,128,256]{1,2,0:T(8,128)(2,1)} %stack.2), calls=%async_computation | async-start | bytes 4194304 | tf_op jit(solution)/shard_map/all_to_all | solution.py:111
  30.9 4.5 compare_select_fusion.1
  35.3 16.2 %select_compare_fusion = pred[4096]{0:T(1024)(128)(4,1)S(1)} fusion(pred[4096]{0:T(1024)(128)(4,1)S(1)} %compare_reduce_fusion, pred[4096]{0:T(1024)(128)(4,1)S(1)} %compare_reduce_fusion.1, pred[4096]{0:T(1024)(128)(4,1)S(1)} %compare_reduce_fusion.2, pred[4096]{0:T(1024)(128)(4,1)S(1)} %compare_reduce_fusion.3, ...), kind=kLoop, calls=%fused_computation.99 | loop fusion | flops 106496 | bytes 122984 | tf_op jit(solution)/shard_map/eq | solution.py:117
  55.7 15.7 %reduce-window.6 = s32[32,8,128]{2,1,0:T(8,128)S(1)} reduce-window(s32[32,8,128]{2,1,0:T(8,128)} %fusion.37, s32[]{:T(128)} %copy.75), window={size=1x1x128 pad=0_0x0_0x127_0}, to_apply=%region_7.8 | reduce-window | flops 4161536 | bytes 262148 | tf_op jit(solution)/shard_map/reduce-window
  81.7 41.2 %all-gather.3.cloned.1.call-done = bf16[4096,256]{1,0:T(8,128)(2,1)} async-done(((bf16[128,256]{1,0:T(8,128)(2,1)}), bf16[4096,256]{1,0:T(8,128)(2,1)}) %all-gather.3.cloned.1.call-update) | async-done | bytes 2097168 | tf_op jit(solution)/shard_map/all_gather | solution.py:109
  122.9 4.0 reshape.358
  126.9 3.4 copy.37
  130.3 6.1 %all-to-all-done = bf16[32,128,256]{1,2,0:T(8,128)(2,1)S(1)} async-done(((bf16[32,128,256]{1,2,0:T(8,128)(2,1)}), bf16[32,128,256]{1,2,0:T(8,128)(2,1)S(1)}, u32[]{:S(2)}, u32[]{:S(2)}) %all-to-all-start) | async-done | bytes 2097184 | tf_op jit(solution)/shard_map/all_to_all | solution.py:111
  136.4 2.7 copy.36
  139.1 3.1 reshape_reshape_reshape.3
  142.2 3.0 copy.39
  145.3 23.7 %while.15 = (s32[]{:T(128)}, f32[2,8,128]{2,1,0:T(8,128)S(1)}, f32[2,8,128]{2,1,0:T(8,128)S(1)}, f32[2,8,128,128]{3,2,1,0:T(8,128)S(1)}, pred[8,512]{1,0:T(8,128...) while((s32[]{:T(128)}, f32[2,8,128]{2,1,0:T(8,128)S(1)}, ...), condition=%wide.region_6.7_spmd.clone, body=%wide.region_0.6_spmd.clone.sunk | while | flops 551227520 | bytes 16131831 | solution.py:63
  147.6 5.4 conditional.3
  150.3 2.6 fusion.8
  169.9 35.4 %all-gather.5.cloned.1.call-done = bf16[2048,1024]{1,0:T(8,128)(2,1)} async-done(((bf16[64,1024]{1,0:T(8,128)(2,1)}), bf16[2048,1024]{1,0:T(8,128)(2,1)}) %all-gather.5.cloned.1.call-update) | async-done | bytes 4194320 | tf_op jit(solution)/shard_map/all_gather | solution.py:128
  205.3 3.0 multiply_reduce_fusion
  209.1 14.9 %scatter_custom_fusion = bf16[1536,1024]{1,0:T(8,128)(2,1)} fusion(s32[1024]{0:T(1024)S(1)} %bitcast.130, bf16[128,1024]{1,0:T(8,128)(2,1)S(1)} %get-tuple-element.206, s32[1024]{0:T(1024)S(1)} %broadcast_clamp_fusion.1, bf16[]{:T(256)} %constant.107.clone.1), kind=kCustom, calls=%fused_computation.34 | custom fusion | bytes 3145730 | tf_op jit(solution)/shard_map/scatter | solution.py:146
  224.0 154.0 %all_to_all.15 = bf16[32,48,1024]{2,1,0:T(8,128)(2,1)S(1)} all-to-all(bf16[32,48,1024]{2,1,0:T(8,128)(2,1)} %bitcast.117), channel_id=1, replica_groups=mesh['pack'=16,'seq'=32] {'seq'}, dimensions={0} | all-to-all | bytes 6291456 | tf_op jit(solution)/shard_map/all_to_all | solution.py:149
  379.7 3.3 fusion.31
  383.0 7.8 %convolution_convert_fusion = bf16[1536,1024]{1,0:T(8,128)(2,1)} fusion(bf16[1536,1024]{1,0:T(8,128)(2,1)} %bitcast.120, f32[1536,384]{1,0:T(8,128)} %fusion.31, bf16[1,384,1024]{2,1,0:T(8,128)(2,1)S(1)} %copy-done, bf16[1,1024,384]{2,1,0:T(8,128)(2,1)S(1)} %copy-done.11), kind=kOutput, calls=%fused_computation.31 | convolution fusion | flops 2421030912 | bytes 10223616 | tf_op jit(solution)/shard_map/dot_general | solution.py:81
  390.8 4.9 all-to-all-start.2
  395.8 146.3 %all-to-all-done.2 = bf16[32,48,1024]{2,1,0:T(8,128)(2,1)} async-done(((bf16[32,48,1024]{2,1,0:T(8,128)(2,1)}), bf16[32,48,1024]{2,1,0:T(8,128)(2,1)}, u32[]{:S(2)}, u32[]{:S(2)}) %all-to-all-start.2) | async-done | bytes 3145760 | tf_op jit(solution)/shard_map/all_to_all | solution.py:151
  542.1 7.3 %gather_fusion = bf16[1024,1024]{1,0:T(8,128)(2,1)S(1)} fusion(bf16[1536,1024]{1,0:T(8,128)(2,1)} %bitcast.54, s32[1024]{0:T(1024)S(1)} %broadcast_clamp_fusion), kind=kCustom, calls=%fused_computation.1 | custom fusion | bytes 4198400 | tf_op jit(solution)/shard_map/gather | solution.py:152
  549.4 2.0 fusion.22
  (134 shorter events, 41.4 us)
Async XLA Ops:
  7.2 375.8 %copy-start = (bf16[1,384,1024]{2,1,0:T(8,128)(2,1)S(1)}, bf16[1,384,1024]{2,1,0:T(8,128)(2,1)}, u32[]{:S(2)}) copy-start(bf16[1,384,1024]{2,1,0:T(8,128)(2,1)} %param.24) | copy-start | bytes 2359300
  7.2 115.7 %all-gather.3.cloned.1.call-start = ((), (), s32[]{:S(2)}) async-start(), calls=%async_computation.3 | async-start | bytes 2162688 | tf_op jit(solution)/shard_map/all_gather | solution.py:109
  8.9 18.2 %copy-start.7 = (s32[128,8]{0,1:T(8,128)S(1)}, s32[128,8]{0,1:T(8,128)}, u32[]{:S(2)}) copy-start(s32[128,8]{0,1:T(8,128)} %param.25) | copy-start | bytes 12292
  8.9 20.5 %copy-start.3 = (s32[32]{0:T(128)S(1)}, s32[32]{0:T(128)}, u32[]{:S(2)}) copy-start(s32[32]{0:T(128)} %param.27) | copy-start | bytes 388
  8.9 43.2 %copy-start.4 = (bf16[128,2048]{1,0:T(8,128)(2,1)S(1)}, bf16[128,2048]{1,0:T(8,128)(2,1)}, u32[]{:S(2)}) copy-start(bf16[128,2048]{1,0:T(8,128)(2,1)} %param.16) | copy-start | bytes 1572868
  10.7 43.8 %copy-start.9 = (bf16[1024]{0:T(1024)(128)(2,1)S(1)}, bf16[1024]{0:T(1024)(128)(2,1)}, u32[]{:S(2)}) copy-start(bf16[1024]{0:T(1024)(128)(2,1)} %param.21) | copy-start | bytes 6148
  10.7 125.7 %all-to-all-start = ((bf16[32,128,256]{1,2,0:T(8,128)(2,1)}), bf16[32,128,256]{1,2,0:T(8,128)(2,1)S(1)}, u32[]{:S(2)}, u32[]{:S(2)}) async-start(bf16[32,128,256]{1,2,0:T(8,128)(2,1)} %stack.2), calls=%async_computation | async-start | bytes 4194304 | tf_op jit(solution)/shard_map/all_to_all | solution.py:111
  26.3 179.0 %all-gather.5.cloned.1.call-start = ((), (), s32[]{:S(2)}) async-start(), calls=%async_computation.4 | async-start | bytes 4325376 | tf_op jit(solution)/shard_map/all_gather | solution.py:128
  169.0 36.3 %copy-start.5 = (bf16[128,1024]{1,0:T(8,128)(2,1)S(1)}, bf16[128,1024]{1,0:T(8,128)(2,1)}, u32[]{:S(2)}) copy-start(bf16[128,1024]{1,0:T(8,128)(2,1)} %param.19) | copy-start | bytes 786436
  169.7 38.6 %copy-start.6 = (f32[1024]{0:T(1024)S(1)}, f32[1024]{0:T(1024)}, u32[]{:S(2)}) copy-start(f32[1024]{0:T(1024)} %convert_element_type.59) | copy-start | bytes 12292
  169.9 39.2 %copy-start.2 = (bf16[16,8,16,128]{3,1,2,0:T(8,128)(2,1)}, bf16[16,8,16,128]{3,1,2,0:T(8,128)(2,1)S(1)}, u32[]{:S(2)}) copy-start(bf16[16,8,16,128]{3,1,2,0:T(8,128)(2,1)S(1)} %copy.56) | copy-start | bytes 1572868
  224.0 155.7 %copy-start.10 = (bf16[1,1024,384]{2,1,0:T(8,128)(2,1)S(1)}, bf16[1,1024,384]{2,1,0:T(8,128)(2,1)}, u32[]{:S(2)}) copy-start(bf16[1,1024,384]{2,1,0:T(8,128)(2,1)} %param.22) | copy-start | bytes 2359300
  378.0 1.7 copy-start.1
  379.7 3.3 copy-start.11
  390.8 5.0 copy-start.8
  390.8 151.3 %all-to-all-start.2 = ((bf16[32,48,1024]{2,1,0:T(8,128)(2,1)}), bf16[32,48,1024]{2,1,0:T(8,128)(2,1)}, u32[]{:S(2)}, u32[]{:S(2)}) async-start(bf16[32,48,1024]{2,1,0:T(8,128)(2,1)} %bitcast.118), calls=%async_computation.2 | async-start | bytes 6291456 | tf_op jit(solution)/shard_map/all_to_all | solution.py:151
Sparse Core Ops, SparseCore 0:
  10.1 112.7 all-gather.2
  125.0 80.2 all-gather.4
